TPU v7x, 256 devices: a whole 4x4x8 slice. The times are simulated.
256 devices in a mesh: row: 16 (over z_hi, x), col: 16 (over y, z_lo, core).
Axes of the slice: x: 4, y: 4, z: 8 (z_hi: 4, z_lo: 2; z = z_hi * 2 + z_lo), core: 2. Of those that a mesh axis runs over, the one named last changes fastest.
Arguments:
- panels: int32 [1], replicated, may hold values from 0 to 15
- inverse: float32 [16384, 16384], P('row', 'col'), may hold values from -4 to 28, as said below
- weight: float32 [1024, 16384], P('row', 'col'), may hold values from -0.046875 to 0.046875
- tokens: bfloat16 [2048, 16384], P('row', 'col'), may hold values from -6 to 6
- targets: bfloat16 [2048, 1024], P('row', 'col'), may hold values from -6 to 6
Outputs:
- new_inverse: float32 [16384, 16384], P('row', 'col')
- pruned: float32 [1024, 16384], P('row', 'col')
- residual: float32 [2048, 1024], P('row', 'col')
- correlation: float32 [1024, 16384], P('row', 'col')
Inputs may be any that keep to these rules, and one draw needn't show every extreme that they name: `inverse`: symmetric and positive definite.
All inputs are finite; a program needn't handle non-finite values.
Results may differ from a plain program's by a relative error of at most 0.0035.
Values may be sent and summed in bfloat16 or wider, within the bound.
A program may use at most 128 MiB of HBM per device.

v0:
```python
import math
import jax
import jax.numpy as jnp
from jax import lax
from jax.sharding import PartitionSpec as P

PW = 1024


def broadcast(array, axis, root):
    mine = lax.axis_index(axis) == root
    return lax.psum(jnp.where(mine, array, jnp.zeros_like(array)), axis)


def cholesky_apply(factor, right_side):
    halfway = lax.linalg.triangular_solve(
        factor, right_side, left_side=True, lower=True, transpose_a=False
    )
    return lax.linalg.triangular_solve(
        factor, halfway, left_side=True, lower=True, transpose_a=True
    )


def shards(panels, inverse, weight, tokens, targets):
    highest = lax.Precision.HIGHEST
    rows_local = inverse.shape[0]
    cols_local = inverse.shape[1]
    out_local = targets.shape[1]
    anchor = panels[0] * PW
    owner_col = anchor // cols_local
    owner_row = anchor // rows_local
    holds_panel = lax.axis_index("col") == owner_col
    col_slab = inverse
    weight_slab = weight
    col_slab = jnp.where(holds_panel, col_slab, jnp.zeros_like(col_slab))
    weight_slab = jnp.where(holds_panel, weight_slab, jnp.zeros_like(weight_slab))
    col_share, weight_share = (
        lax.psum_scatter(col_slab, "col", scatter_dimension=0, tiled=True),
        lax.psum_scatter(weight_slab, "col", scatter_dimension=0, tiled=True),
    )
    col_slab, weight_slab = (
        lax.all_gather(col_share, "col", axis=0, tiled=True),
        lax.all_gather(weight_share, "col", axis=0, tiled=True),
    )
    is_owner = lax.axis_index("row") == owner_row
    safe_block = jnp.where(is_owner, col_slab, jnp.eye(PW, dtype=jnp.float32))
    factor = jnp.linalg.cholesky(safe_block)
    solved = cholesky_apply(factor, inverse)
    solved = broadcast(solved, "row", owner_row)
    new_inverse = inverse - jnp.dot(
        col_slab, solved, precision=highest, preferred_element_type=jnp.float32
    )
    pruned = weight - jnp.dot(
        weight_slab, solved, precision=highest, preferred_element_type=jnp.float32
    )
    pruned_low = pruned.astype(jnp.bfloat16)
    partial_value = lax.dot_general(
        tokens,
        lax.all_gather(pruned_low, "row", axis=0, tiled=True),
        (((1,), (1,)), ((), ())),
        preferred_element_type=jnp.float32,
    )
    col_index = lax.axis_index("col")
    placed = lax.dynamic_update_slice_in_dim(
        jnp.zeros_like(partial_value), targets.astype(jnp.float32), col_index * out_local, 1
    )
    partial_value = partial_value - placed
    residual = lax.psum_scatter(partial_value, "col", scatter_dimension=1, tiled=True)
    residual_low = lax.all_gather(residual.astype(jnp.bfloat16), "col", axis=1, tiled=True)
    token_count = tokens.shape[0] * lax.axis_size("row")
    correlation = lax.psum_scatter(
        lax.dot_general(
            residual_low, tokens, (((0,), (0,)), ((), ())), preferred_element_type=jnp.float32
        ),
        "row",
        scatter_dimension=0,
        tiled=True,
    )
    correlation = correlation * (1.0 / math.sqrt(token_count))
    return (new_inverse, pruned, residual, correlation)


def solution(mesh):
    in_specs = (P(), P("row", "col"), P("row", "col"), P("row", "col"), P("row", "col"))
    out_specs = (P("row", "col"), P("row", "col"), P("row", "col"), P("row", "col"))
    return jax.shard_map(shards, mesh=mesh, in_specs=in_specs, out_specs=out_specs, check_vma=False)
```

profile of v0, /device:TPU:8, one launch (start us, length us, event | category | flops | bytes accessed | tf_op | source)
XLA Modules:
  0.0 1028.7 jit_solution(10012692551235183180)
XLA Ops:
  21.5 70.3 %reduce-scatter.10.cloned.1.call-done = f32[64,1024]{1,0:T(8,128)} async-done(((f32[1024,1024]{1,0:T(8,128)}), f32[64,1024]{1,0:T(8,128)}) %reduce-scatter.10.cloned.1.call-update) | async-done | bytes 262160 | tf_op jit(solution)/shard_map/reduce_scatter | solution.py:38
  92.8 45.8 %all-gather.4.cloned.1.call-done = f32[1024,1024]{1,0:T(8,128)} async-done(((f32[64,1024]{1,0:T(8,128)}), f32[1024,1024]{1,0:T(8,128)}) %all-gather.4.cloned.1.call-update) | async-done | bytes 4194320 | tf_op jit(solution)/shard_map/all_gather | solution.py:42
  157.5 11.7 %cholesky.222 = f32[128,128]{1,0:T(8,128)S(1)} custom-call(f32[128,128]{1,0:T(8,128)S(1)} %cholesky.577), custom_call_target="Cholesky" | custom-call | tf_op jit(solution)/shard_map/jit(cholesky)/cholesky | solution.py:47
  169.3 9.8 custom-call.64
  182.2 11.7 %cholesky.243 = f32[128,128]{1,0:T(8,128)S(1)} custom-call(f32[128,128]{1,0:T(8,128)S(1)} %cholesky.581), custom_call_target="Cholesky" | custom-call | tf_op jit(solution)/shard_map/jit(cholesky)/cholesky | solution.py:47
  194.6 9.8 custom-call.65
  209.9 11.7 %cholesky.466 = f32[128,128]{1,0:T(8,128)S(1)} custom-call(f32[128,128]{1,0:T(8,128)S(1)} %cholesky.586), custom_call_target="Cholesky" | custom-call | tf_op jit(solution)/shard_map/jit(cholesky)/cholesky | solution.py:47
  222.4 9.8 custom-call.66
  237.0 11.7 %cholesky.485 = f32[128,128]{1,0:T(8,128)S(1)} custom-call(f32[128,128]{1,0:T(8,128)S(1)} %cholesky.591), custom_call_target="Cholesky" | custom-call | tf_op jit(solution)/shard_map/jit(cholesky)/cholesky | solution.py:47
  249.5 9.8 custom-call.67
  263.6 11.9 %cholesky.504 = f32[128,128]{1,0:T(8,128)S(1)} custom-call(f32[128,128]{1,0:T(8,128)S(1)} %cholesky.596), custom_call_target="Cholesky" | custom-call | tf_op jit(solution)/shard_map/jit(cholesky)/cholesky | solution.py:47
  276.2 9.8 custom-call.68
  290.3 11.7 %cholesky.524 = f32[128,128]{1,0:T(8,128)S(1)} custom-call(f32[128,128]{1,0:T(8,128)S(1)} %cholesky.601), custom_call_target="Cholesky" | custom-call | tf_op jit(solution)/shard_map/jit(cholesky)/cholesky | solution.py:47
  316.6 11.7 %cholesky.544 = f32[128,128]{1,0:T(8,128)S(1)} custom-call(f32[128,128]{1,0:T(8,128)S(1)} %cholesky.606), custom_call_target="Cholesky" | custom-call | tf_op jit(solution)/shard_map/jit(cholesky)/cholesky | solution.py:47
  342.0 11.7 %cholesky.562 = f32[128,128]{1,0:T(8,128)S(1)} custom-call(f32[128,128]{1,0:T(8,128)S(1)} %convolution_subtract_fusion.18), custom_call_target="Cholesky" | custom-call | tf_op jit(solution)/shard_map/jit(cholesky)/cholesky | solution.py:47
  368.8 23.9 %while.1 = (s32[]{:T(128)}, f32[1024,1024]{0,1:T(8,128)}, s32[8,2]{0,1:T(2,128)S(1)}, f32[8,128,128]{2,1,0:T(8,128)S(1)}, s32[]{:T(128)}) while((s32[]{:T(128)}, f32[1024,1024]{0,1:T(8,128)}, s32[8,2]{0,1:T(2,128)S(1)}, f32[8,128,128]{2,1,0:T(8,128)S(1)}, s32[]{:T(128)}) %tuple.55), condition=%wide.while_cond, body=%wide.while_body.sunk | while | flops 2 | bytes 393321 | solution.py:19
  392.7 78.8 %custom-call.71 = f32[8,128,128]{1,2,0:T(8,128)S(1)} custom-call(f32[8,128,128]{2,1,0:T(8,128)S(1)} %get-tuple-element.11), custom_call_target="InvertDiagBlocksLowerTriangular" | custom-call | tf_op jit(solution)/shard_map/triangular_solve | solution.py:19
  550.8 17.1 %all-gather = f32[16,4,1024]{2,1,0:T(4,128)S(1)} all-gather(f32[1,4,1024]{2,1,0:T(4,128)S(1)} %dynamic-slice_bitcast_fusion), channel_id=1, replica_groups=mesh['row'=16,'col'=16] {'col'}, dimensions={0}, use_global_device_ids=true | all-gather | bytes 278528 | tf_op jit(solution)/shard_map/all_gather | solution.py:43
  568.0 207.9 %all-reduce.5.cloned.1.call-done = f32[1024,1024]{0,1:T(8,128)} async-done(((f32[1024,1024]{0,1:T(8,128)}), f32[1024,1024]{0,1:T(8,128)}) %all-reduce.5.cloned.1.call-update) | async-done | bytes 4194320 | tf_op jit(solution)/shard_map/psum | solution.py:12
  783.1 56.1 %all-gather.6.cloned.1.call-done = bf16[1024,1024]{1,0:T(8,128)(2,1)} async-done(((bf16[64,1024]{1,0:T(8,128)(2,1)}), bf16[1024,1024]{1,0:T(8,128)(2,1)}) %all-gather.6.cloned.1.call-update) | async-done | bytes 2097168 | tf_op jit(solution)/shard_map/all_gather | solution.py:59
  842.3 55.6 %reduce-scatter.6.cloned.1.call-done = f32[128,64]{0,1:T(8,128)} async-done(((f32[128,1024]{0,1:T(8,128)}), f32[128,64]{0,1:T(8,128)}) %reduce-scatter.6.cloned.1.call-update) | async-done | bytes 32784 | tf_op jit(solution)/shard_map/reduce_scatter | solution.py:68
  898.6 21.7 %all_gather.15 = bf16[128,1024]{0,1:T(8,128)(2,1)S(1)} all-gather(bf16[128,64]{0,1:T(8,128)(2,1)S(1)} %convert_element_type.15), channel_id=1, replica_groups=mesh['row'=16,'col'=16] {'col'}, dimensions={1}, use_global_device_ids=true | all-gather | bytes 278528 | tf_op jit(solution)/shard_map/all_gather | solution.py:69
  923.1 18.4 %convolution_subtract_fusion = f32[1024,1024]{1,0:T(8,128)} fusion(f32[1024,1024]{1,0:T(8,128)} %param.6, f32[1024,1024]{1,0:T(8,128)} %all-gather.4.cloned.1.call-done, f32[1024,1024]{0,1:T(8,128)} %all-reduce.5.cloned.1.call-done), kind=kOutput, calls=%fused_computation.26 | convolution fusion | flops 12885950464 | bytes 16777216 | tf_op jit(solution)/shard_map/dot_general | solution.py:50
  941.4 78.6 %reduce-scatter.8.cloned.1.call-done = f32[64,1024]{1,0:T(8,128)} async-done(((f32[1024,1024]{1,0:T(8,128)}), f32[64,1024]{1,0:T(8,128)}) %reduce-scatter.8.cloned.1.call-update) | async-done | bytes 262160 | tf_op jit(solution)/shard_map/reduce_scatter | solution.py:71
  (231 shorter events, 213.9 us)
Async XLA Ops:
  7.2 832.0 %copy-start = (bf16[128,1024]{1,0:T(8,128)(2,1)S(1)}, bf16[128,1024]{1,0:T(8,128)(2,1)}, u32[]{:S(2)}) copy-start(bf16[128,1024]{1,0:T(8,128)(2,1)} %param.8) | copy-start | bytes 786436
  7.2 84.7 %reduce-scatter.10.cloned.1.call-start = ((), (), s32[]{:S(2)}) async-start(), calls=%async_computation.8 | async-start | bytes 4456448 | tf_op jit(solution)/shard_map/reduce_scatter | solution.py:38
  21.5 70.5 %copy-start.15 = (f32[64,1024]{1,0:T(8,128)S(1)}, f32[64,1024]{1,0:T(8,128)}, u32[]{:S(2)}) copy-start(f32[64,1024]{1,0:T(8,128)} %param.7) | copy-start | bytes 786436
  21.5 117.1 %all-gather.4.cloned.1.call-start = ((), (), s32[]{:S(2)}) async-start(), calls=%async_computation.3 | async-start | bytes 4456448 | tf_op jit(solution)/shard_map/all_gather | solution.py:42
  91.9 458.1 %all-reduce.7.cloned.1.call-start = ((), (), s32[]{:S(2)}) async-start(), calls=%async_computation.9 | async-start | bytes 524288
  92.7 683.2 %all-reduce.5.cloned.1.call-start = ((), (), s32[]{:S(2)}) async-start(), calls=%async_computation.4 | async-start | bytes 8388608 | tf_op jit(solution)/shard_map/psum | solution.py:12
  155.5 2.0 copy-start.4
  471.4 23.6 %copy-start.14 = (f32[8,128,128]{1,2,0:T(8,128)}, f32[8,128,128]{1,2,0:T(8,128)S(1)}, u32[]{:S(2)}) copy-start(f32[8,128,128]{1,2,0:T(8,128)S(1)} %custom-call.71) | copy-start | bytes 1572868
  471.4 4.4 copy-start.2
  475.2 3.6 copy-start.3
  475.9 4.8 copy-start.5
  478.8 3.2 copy-start.7
  509.9 4.2 copy-start.6
  527.4 9.0 copy-start.8
  529.1 12.0 %copy-start.13 = (f32[128,1024]{0,1:T(8,128)S(1)}, f32[128,1024]{0,1:T(8,128)}, u32[]{:S(2)}) copy-start(f32[128,1024]{0,1:T(8,128)} %copy.58) | copy-start | bytes 1572868
  529.1 12.9 %copy-start.12 = (f32[128,1024]{0,1:T(8,128)S(1)}, f32[128,1024]{0,1:T(8,128)}, u32[]{:S(2)}) copy-start(f32[128,1024]{0,1:T(8,128)} %copy.59) | copy-start | bytes 1572868
  533.6 9.2 copy-start.11
  533.6 10.0 copy-start.10
  533.6 10.8 %copy-start.9 = (f32[128,1024]{0,1:T(8,128)S(1)}, f32[128,1024]{0,1:T(8,128)}, u32[]{:S(2)}) copy-start(f32[128,1024]{0,1:T(8,128)} %copy.62) | copy-start | bytes 1572868
  548.1 227.9 %copy-start.16 = (f32[64,1024]{1,0:T(8,128)S(1)}, f32[64,1024]{1,0:T(8,128)}, u32[]{:S(2)}) copy-start(f32[64,1024]{1,0:T(8,128)} %param.7) | copy-start | bytes 786436
  548.1 235.0 %copy-start.17 = (bf16[128,64]{0,1:T(8,128)(2,1)S(1)}, bf16[128,64]{0,1:T(8,128)(2,1)}, u32[]{:S(2)}) copy-start(bf16[128,64]{0,1:T(8,128)(2,1)} %param.9) | copy-start | bytes 49156
  548.1 291.0 %all-gather.6.cloned.1.call-start = ((), (), s32[]{:S(2)}) async-start(), calls=%async_computation.5 | async-start | bytes 2228224 | tf_op jit(solution)/shard_map/all_gather | solution.py:59
  783.0 114.9 %reduce-scatter.6.cloned.1.call-start = ((), (), s32[]{:S(2)}) async-start(), calls=%async_computation.6 | async-start | bytes 557056 | tf_op jit(solution)/shard_map/reduce_scatter | solution.py:68
  842.3 177.7 %reduce-scatter.8.cloned.1.call-start = ((), (), s32[]{:S(2)}) async-start(), calls=%async_computation.7 | async-start | bytes 4456448 | tf_op jit(solution)/shard_map/reduce_scatter | solution.py:71
  (2 other events, 2.6 us)
Sparse Core Ops, SparseCore 0:
  21.6 70.2 reduce-scatter.9
  93.7 44.8 all-gather.3
  141.8 118.2 all-reduce.6
  548.2 227.6 all-reduce.4
  783.1 56.0 all-gather.5
  842.4 55.4 reduce-scatter.5
  923.2 96.8 reduce-scatter.7
where the time goes:
time: 1030 us
  waiting for transfers between devices  514 us (50%)
  other arithmetic  266 us (26%)
  matrix products  104 us (10%)
  local copies, waits for them, and re-layouts  83.4 us (8%)
  blocking collectives  38.9 us (4%)
  between operations  21.3 us (2%)
    psum x1, waiting for transfers between devices, broadcast(): return lax.psum(jnp.where(mine, array, jnp.zeros_like(array)), axis)  208 us
    another operation x30, other arithmetic, shards(): factor = jnp.linalg.cholesky(safe_block)  167 us
    another operation x3, other arithmetic, cholesky_apply(): lax.linalg.triangular_solve(factor, halfway, left_side=True, lower=True,...  83.7 us
    reduce_scatter x1, waiting for transfers between devices, shards(): lax.psum_scatter(lax.dot_general(residual_low, tokens, (((0,), (0,)), (()...  78.6 us
    reduce_scatter x1, waiting for transfers between devices, shards(): lax.psum_scatter(col_slab, 'col', scatter_dimension=0, tiled=True)  70.3 us
    all_gather x1, waiting for transfers between devices, shards(): lax.all_gather(pruned_low, 'row', axis=0, tiled=True)  56.1 us
    reduce_scatter x1, waiting for transfers between devices, shards(): lax.psum_scatter(partial_value, 'col', scatter_dimension=1, tiled=True)  55.6 us
    all_gather x1, waiting for transfers between devices, shards(): lax.all_gather(col_share, 'col', axis=0, tiled=True)  45.8 us
  transfers between devices with their start and end apart: 7, of which 6 were waited for; matrix products, arithmetic and copies ran while one was open for 41% of the time, Pallas kernels for 0%

commit v1 on v0

--- a/solution.py
+++ b/solution.py
@@ -9,7 +9,7 @@
 
 def broadcast(array, axis, root):
     mine = lax.axis_index(axis) == root
-    return lax.psum(jnp.where(mine, array, jnp.zeros_like(array)), axis)
+    return jnp.sum(lax.all_gather(jnp.where(mine, array, jnp.zeros_like(array)), axis), axis=0)
 
 
 def cholesky_apply(factor, right_side):

time: 1030 us -> 1500 us (1.46)
  waiting for transfers between devices: 514 us -> 1010 us
  local copies, waits for them, and re-layouts: 83.4 us -> 42.2 us
  other arithmetic: 266 us -> 294 us
  matrix products: 104 us -> 85.9 us
    all_gather x0 -> x1, waiting for transfers between devices: none -> 697 us  [broadcast(): lax.all_gather(jnp.where(mine, array, jnp.zeros_like(array)), axis)]
    psum x1 -> x0, waiting for transfers between devices: 208 us -> none  [broadcast(): return lax.psum(jnp.where(mine, array, jnp.zeros_like(array)), axis)]
    unnamed x61 -> x35, local copies, waits for them, and re-layouts: 32.6 us -> 4.76 us
    reduce_sum x0 -> x1, other arithmetic: none -> 22.9 us  [broadcast(): jnp.sum(lax.all_gather(jnp.where(mine, array, jnp.zeros_like(array)), axi...]
  transfers between devices with their start and end apart: 7 -> 7, of which waited for: 6 -> 6; matrix products, arithmetic and copies ran while one was open for 41% -> 25% of each run, Pallas kernels for 0% -> 0%
where the time goes in v1:
time: 1500 us; the launch traced here: 1490 us
  waiting for transfers between devices  1010 us (67%)
  other arithmetic  294 us (20%)
  matrix products  85.9 us (6%)
  local copies, waits for them, and re-layouts  42.2 us (3%)
  blocking collectives  38.9 us (3%)
  between operations  21.3 us (1%)
    all_gather x1, waiting for transfers between devices, broadcast(): lax.all_gather(jnp.where(mine, array, jnp.zeros_like(array)), axis)  697 us
    another operation x30, other arithmetic, shards(): factor = jnp.linalg.cholesky(safe_block)  173 us
    another operation x3, other arithmetic, cholesky_apply(): lax.linalg.triangular_solve(factor, halfway, left_side=True, lower=True,...  83.7 us
    reduce_scatter x1, waiting for transfers between devices, shards(): lax.psum_scatter(lax.dot_general(residual_low, tokens, (((0,), (0,)), (()...  78.5 us
    reduce_scatter x1, waiting for transfers between devices, shards(): lax.psum_scatter(col_slab, 'col', scatter_dimension=0, tiled=True)  70.2 us
    all_gather x1, waiting for transfers between devices, shards(): lax.all_gather(pruned_low, 'row', axis=0, tiled=True)  60.8 us
    reduce_scatter x1, waiting for transfers between devices, shards(): lax.psum_scatter(partial_value, 'col', scatter_dimension=1, tiled=True)  55.5 us
    all_gather x1, waiting for transfers between devices, shards(): lax.all_gather(col_share, 'col', axis=0, tiled=True)  46.1 us
  transfers between devices with their start and end apart: 7, of which 6 were waited for; matrix products, arithmetic and copies ran while one was open for 25% of the time, Pallas kernels for 0%

profile of v1, /device:TPU:8, one launch (start us, length us, event | category | flops | bytes accessed | tf_op | source)
XLA Modules:
  0.0 1491.2 jit_solution(4839549526985690824)
XLA Ops:
  10.9 70.2 %reduce-scatter.10.cloned.1.call-done = f32[64,1024]{1,0:T(8,128)} async-done(((f32[1024,1024]{1,0:T(8,128)}), f32[64,1024]{1,0:T(8,128)}) %reduce-scatter.10.cloned.1.call-update) | async-done | bytes 262160 | tf_op jit(solution)/shard_map/reduce_scatter | solution.py:38
  82.0 46.1 %all-gather.5.cloned.1.call-done = f32[1024,1024]{1,0:T(8,128)} async-done(((f32[64,1024]{1,0:T(8,128)}), f32[1024,1024]{1,0:T(8,128)}) %all-gather.5.cloned.1.call-update) | async-done | bytes 4194320 | tf_op jit(solution)/shard_map/all_gather | solution.py:42
  146.7 11.7 cholesky.222
  161.0 9.8 custom-call.64
  174.7 12.2 cholesky.243
  200.6 11.7 cholesky.466
  226.9 11.9 cholesky.485
  240.1 9.8 custom-call.67
  253.3 11.7 cholesky.504
  266.4 10.0 custom-call.68
  279.7 11.7 cholesky.524
  292.6 9.8 custom-call.69
  305.5 12.1 cholesky.544
  331.3 11.7 cholesky.562
  354.9 24.1 %while.1 = (s32[]{:T(128)}, f32[1024,1024]{1,0:T(8,128)}, s32[8,2]{0,1:T(2,128)S(1)}, f32[8,128,128]{2,1,0:T(8,128)S(1)}, s32[]{:T(128)}) while((s32[]{:T(128)}, f32[1024,1024]{1,0:T(8,128)}, s32[8,2]{0,1:T(2,128)S(1)}, f32[8,128,128]{2,1,0:T(8,128)S(1)}, s32[]{:T(128)}) %tuple.62), condition=%wide.while_cond, body=%wide.while_body.sunk | while | flops 2 | bytes 131181 | solution.py:19
  379.0 78.8 %custom-call.71 = f32[8,128,128]{1,2,0:T(8,128)S(1)} custom-call(f32[8,128,128]{2,1,0:T(8,128)S(1)} %get-tuple-element.11), custom_call_target="InvertDiagBlocksLowerTriangular" | custom-call | tf_op jit(solution)/shard_map/triangular_solve | solution.py:19
  497.6 17.1 %all-gather = f32[16,4,1024]{2,1,0:T(4,128)S(1)} all-gather(f32[1,4,1024]{2,1,0:T(4,128)S(1)} %dynamic-slice_bitcast_fusion), channel_id=1, replica_groups=mesh['row'=16,'col'=16] {'col'}, dimensions={0}, use_global_device_ids=true | all-gather | bytes 278528 | tf_op jit(solution)/shard_map/all_gather | solution.py:43
  514.8 697.4 %all-gather.7.cloned.1.call-done = f32[16,1024,1024]{2,1,0:T(8,128)} async-done(((f32[1,1024,1024]{2,1,0:T(8,128)}), f32[16,1024,1024]{2,1,0:T(8,128)}) %all-gather.7.cloned.1.call-update) | async-done | bytes 67108880 | tf_op jit(solution)/shard_map/all_gather | solution.py:12
  1212.3 22.9 %reduce_sum.9 = f32[1024,1024]{1,0:T(8,128)} reduce(f32[16,1024,1024]{2,1,0:T(8,128)} %all-gather.7.cloned.1.call-done, f32[]{:T(128)} %constant.302.clone.1), dimensions={0}, to_apply=%region_17.18 | reduce | flops 15728640 | bytes 71303168 | tf_op jit(solution)/shard_map/reduce_sum | solution.py:12
  1240.9 60.8 %all-gather.9.cloned.1.call-done = bf16[1024,1024]{1,0:T(8,128)(2,1)} async-done(((bf16[64,1024]{1,0:T(8,128)(2,1)}), bf16[1024,1024]{1,0:T(8,128)(2,1)}) %all-gather.9.cloned.1.call-update) | async-done | bytes 2097168 | tf_op jit(solution)/shard_map/all_gather | solution.py:59
  1304.9 55.5 %reduce-scatter.6.cloned.1.call-done = f32[128,64]{0,1:T(8,128)} async-done(((f32[128,1024]{0,1:T(8,128)}), f32[128,64]{0,1:T(8,128)}) %reduce-scatter.6.cloned.1.call-update) | async-done | bytes 32784 | tf_op jit(solution)/shard_map/reduce_scatter | solution.py:68
  1361.2 21.8 %all_gather.20 = bf16[128,1024]{0,1:T(8,128)(2,1)S(1)} all-gather(bf16[128,64]{0,1:T(8,128)(2,1)S(1)} %convert_element_type.15), channel_id=1, replica_groups=mesh['row'=16,'col'=16] {'col'}, dimensions={1}, use_global_device_ids=true | all-gather | bytes 278528 | tf_op jit(solution)/shard_map/all_gather | solution.py:69
  1385.6 18.3 %convolution_subtract_fusion = f32[1024,1024]{1,0:T(8,128)} fusion(f32[1024,1024]{1,0:T(8,128)} %param.6, f32[1024,1024]{1,0:T(8,128)} %all-gather.5.cloned.1.call-done, f32[1024,1024]{1,0:T(8,128)} %reduce_sum.9), kind=kOutput, calls=%fused_computation.26 | convolution fusion | flops 12885950464 | bytes 16777216 | tf_op jit(solution)/shard_map/dot_general | solution.py:50
  1404.0 78.5 %reduce-scatter.8.cloned.1.call-done = f32[64,1024]{1,0:T(8,128)} async-done(((f32[1024,1024]{1,0:T(8,128)}), f32[64,1024]{1,0:T(8,128)}) %reduce-scatter.8.cloned.1.call-update) | async-done | bytes 262160 | tf_op jit(solution)/shard_map/reduce_scatter | solution.py:71
  (166 shorter events, 168.1 us)
Async XLA Ops:
  7.2 1294.6 %copy-start = (bf16[128,1024]{1,0:T(8,128)(2,1)S(1)}, bf16[128,1024]{1,0:T(8,128)(2,1)}, u32[]{:S(2)}) copy-start(bf16[128,1024]{1,0:T(8,128)(2,1)} %param.8) | copy-start | bytes 786436
  7.2 73.9 %reduce-scatter.10.cloned.1.call-start = ((), (), s32[]{:S(2)}) async-start(), calls=%async_computation.8 | async-start | bytes 4456448 | tf_op jit(solution)/shard_map/reduce_scatter | solution.py:38
  10.8 70.3 %copy-start.4 = (f32[64,1024]{1,0:T(8,128)S(1)}, f32[64,1024]{1,0:T(8,128)}, u32[]{:S(2)}) copy-start(f32[64,1024]{1,0:T(8,128)} %param.7) | copy-start | bytes 786436
  10.8 117.3 %all-gather.5.cloned.1.call-start = ((), (), s32[]{:S(2)}) async-start(), calls=%async_computation.3 | async-start | bytes 4456448 | tf_op jit(solution)/shard_map/all_gather | solution.py:42
  81.1 415.8 %all-reduce.4.cloned.1.call-start = ((), (), s32[]{:S(2)}) async-start(), calls=%async_computation.9 | async-start | bytes 524288
  81.9 1130.4 %all-gather.7.cloned.1.call-start = ((), (), s32[]{:S(2)}) async-start(), calls=%async_computation.4 | async-start | bytes 71303168 | tf_op jit(solution)/shard_map/all_gather | solution.py:12
  144.8 1.9 copy-start.3
  457.8 4.3 copy-start.1
  461.4 3.4 copy-start.2
  494.9 0.7 copy-start.6
  494.9 806.8 %all-gather.9.cloned.1.call-start = ((), (), s32[]{:S(2)}) async-start(), calls=%async_computation.5 | async-start | bytes 2228224 | tf_op jit(solution)/shard_map/all_gather | solution.py:59
  1235.2 5.7 copy-start.5
  1240.8 119.6 %reduce-scatter.6.cloned.1.call-start = ((), (), s32[]{:S(2)}) async-start(), calls=%async_computation.6 | async-start | bytes 557056 | tf_op jit(solution)/shard_map/reduce_scatter | solution.py:68
  1304.8 177.6 %reduce-scatter.8.cloned.1.call-start = ((), (), s32[]{:S(2)}) async-start(), calls=%async_computation.7 | async-start | bytes 4456448 | tf_op jit(solution)/shard_map/reduce_scatter | solution.py:71
Sparse Core Ops, SparseCore 0:
  11.1 69.9 reduce-scatter.9
  82.9 45.1 all-gather.4
  131.3 118.2 all-reduce.3
  495.1 717.1 all-gather.6
  1240.9 60.7 all-gather.8
  1305.0 55.4 reduce-scatter.5
  1385.7 96.6 reduce-scatter.7
